TPU v7x, 32 devices: a whole 2x2x4 slice. The times are simulated.
32 devices in a mesh: state: 8 (over z, y), member: 4 (over x, core).
Axes of the slice: x: 2, y: 2, z: 4, core: 2. Of those that a mesh axis runs over, the one named last changes fastest.
Arguments:
- anomalies: bfloat16 [64, 256, 1024], P('state', 'member'), may hold values from -6 to 6
- tapers: bfloat16 [2, 1024, 1024], replicated, may hold values from 0 to 1, as said below
- nbr_block: int32 [64, 12], P('state'), may hold values from 0 to 63, as said below
- taper_index: int32 [64, 12], P('state'), may hold values from 0 to 1
- pair_count: int32 [64], P('state'), may hold values from 5 to 12, as said below
- obs_cell: int32 [65536], P('state'), may hold values from 0 to 8191, as said below
- obs_value: float32 [65536], P('state'), may hold values from -3 to 3
Outputs:
- increments: float32 [64, 1024], P('state', 'member')
Inputs may be any that keep to these rules, and one draw needn't show every extreme that they name: `nbr_block`: every slot of block i names a block whose state index (block // 8) lies within 2 of i // 8 around the closed loop of state indices; slot 0 names i itself, and slots 1 to 4 name blocks at state-index offsets -2 to 2 without 0, in rising order. Block i uses slots 0 to pair_count[i] - 1; at least one block uses all 12 slots. Observation r lies in variable obs_cell[r] of the 8192 variables held by state index r // 8192, counted block by block. `tapers`: Gaspari-Cohn taper values of pairs of variables.
All inputs are finite; a program needn't handle non-finite values.
Results may differ from a plain program's by a relative error of at most 0.0018.
Values may be sent and summed in bfloat16 or wider, within the bound.
A program may use at most 64 MiB of HBM per device.

v0:
```python
import jax
import jax.numpy as jnp
from jax import lax
from jax.sharding import PartitionSpec as P

M = 256
HOPS = 2
KT = 2


def from_behind(value, axis, by):
    size = lax.axis_size(axis)
    return lax.ppermute(value, axis, [(i, (i + by) % size) for i in range(size)])


def on_device(anomalies, tapers, nbr_block, taper_index, pair_count, obs_cell, obs_value):
    local_blocks = anomalies.shape[0]
    block_width = anomalies.shape[2]
    slot_total = nbr_block.shape[1]
    own_index = lax.axis_index("state")
    state_count = lax.axis_size("state")
    observation_residual = (
        jnp.zeros((local_blocks * block_width,), jnp.float32).at[obs_cell].add(obs_value)
    )
    observation_residual = observation_residual.reshape(local_blocks, block_width)
    weighted = (anomalies.astype(jnp.float32) * observation_residual[:, None, :]).astype(
        jnp.bfloat16
    )
    current = from_behind(weighted, "state", -HOPS)
    arrived = [current]
    for pass_index in range(2 * HOPS):
        current = from_behind(current, "state", 1)
        arrived.append(current)
    ordered = arrived[::-1]
    panels = jnp.concatenate(ordered, axis=0)
    panel_total = panels.shape[0]
    device_gap = (nbr_block // local_blocks - own_index + HOPS + state_count) % state_count
    position = device_gap * local_blocks + nbr_block % local_blocks
    slot_ids = jnp.arange(slot_total, dtype=jnp.int32)
    is_valid = slot_ids[None, :] < pair_count[:, None]
    tile_ids = jnp.arange(KT, dtype=jnp.int32)
    tile_onehot = (
        (taper_index[:, :, None] == tile_ids[None, None, :]) & is_valid[:, :, None]
    ).astype(jnp.float32)
    place_ids = jnp.arange(panel_total, dtype=jnp.int32)
    place_onehot = (position[:, :, None] == place_ids[None, None, :]).astype(jnp.float32)
    slot_counts = jnp.einsum("lst,lsp->ltp", tile_onehot, place_onehot).astype(jnp.bfloat16)
    gathered_groups = jnp.einsum(
        "ltp,pmb->ltmb", slot_counts, panels, preferred_element_type=jnp.float32
    ).astype(jnp.bfloat16)
    spread = lax.dot_general(
        gathered_groups, tapers, (((1, 3), (0, 2)), ((), ())), preferred_element_type=jnp.float32
    )
    partial_value = jnp.sum(anomalies.astype(jnp.float32) * spread, axis=1) / jnp.float32(M - 1)
    return lax.psum_scatter(partial_value, "member", scatter_dimension=1, tiled=True)


def solution(mesh):
    placed = (
        P("state", "member", None),
        P(),
        P("state", None),
        P("state", None),
        P("state"),
        P("state"),
        P("state"),
    )
    return jax.shard_map(
        on_device, mesh=mesh, in_specs=placed, out_specs=P("state", "member"), check_vma=False
    )
```

profile of v0, /device:TPU:0, one launch (start us, length us, event | category | flops | bytes accessed | tf_op | source)
XLA Modules:
  0.0 218.6 jit_solution(3225720257959662203)
XLA Ops:
  6.5 0.0 reduce-scatter.2.cloned.1.call-start
  6.5 0.8 compare_select_fusion
  7.3 43.4 %scatter_custom_fusion = f32[8192]{0:T(1024)S(1)} fusion(s32[8192]{0:T(1024)S(1)} %compare_select_fusion, f32[8192]{0:T(1024)} %param.13, f32[]{:T(128)} %constant.49.clone.1), kind=kCustom, calls=%fused_computation.20 | custom fusion | flops 8192 | bytes 33280 | tf_op jit(solution)/shard_map/scatter-add | solution.py:23
  50.7 1.5 fusion.4
  52.2 5.1 %collective-permute-start = (bf16[8,64,1024]{2,1,0:T(8,128)(2,1)S(1)}, bf16[8,64,1024]{2,1,0:T(8,128)(2,1)S(1)}, u32[]{:S(2)}, u32[]{:S(2)}) collective-permute-start(bf16[8,64,1024]{2,1,0:T(8,128)(2,1)S(1)} %fusion.4), channel_id=1, source_target_pairs={{0,24},{4,28},{8,0},{12,4},{16,8},{20,12},{24,16},{28,20},{1,25},{... | collective-permute-start | bytes 3145736 | tf_op jit(solution)/shard_map/ppermute | solution.py:13
  57.3 22.4 %collective-permute-done = bf16[8,64,1024]{2,1,0:T(8,128)(2,1)S(1)} collective-permute-done((bf16[8,64,1024]{2,1,0:T(8,128)(2,1)S(1)}, bf16[8,64,1024]{2,1,0:T(8,128)(2,1)S(1)}, u32[]{:S(2)}, u32[]{:S(2)}) %collective-permute-start) | collective-permute-done | bytes 1048608 | tf_op jit(solution)/shard_map/ppermute | solution.py:13
  79.8 2.0 collective-permute-start.1
  81.8 25.5 %collective-permute-done.1 = bf16[8,64,1024]{2,1,0:T(8,128)(2,1)S(1)} collective-permute-done((bf16[8,64,1024]{2,1,0:T(8,128)(2,1)S(1)}, bf16[8,64,1024]{2,1,0:T(8,128)(2,1)S(1)}, u32[]{:S(2)}, u32[]{:S(2)}) %collective-permute-start.1) | collective-permute-done | bytes 1048608 | tf_op jit(solution)/shard_map/ppermute | solution.py:13
  107.3 0.0 collective-permute-start.2
  107.3 25.7 %collective-permute-done.2 = bf16[8,64,1024]{2,1,0:T(8,128)(2,1)S(1)} collective-permute-done((bf16[8,64,1024]{2,1,0:T(8,128)(2,1)S(1)}, bf16[8,64,1024]{2,1,0:T(8,128)(2,1)S(1)}, u32[]{:S(2)}, u32[]{:S(2)}) %collective-permute-start.2) | collective-permute-done | bytes 1048608 | tf_op jit(solution)/shard_map/ppermute | solution.py:13
  133.0 0.0 collective-permute-start.3
  133.0 24.9 %collective-permute-done.3 = bf16[8,64,1024]{2,1,0:T(8,128)(2,1)} collective-permute-done((bf16[8,64,1024]{2,1,0:T(8,128)(2,1)S(1)}, bf16[8,64,1024]{2,1,0:T(8,128)(2,1)}, u32[]{:S(2)}, u32[]{:S(2)}) %collective-permute-start.3) | collective-permute-done | bytes 1048608 | tf_op jit(solution)/shard_map/ppermute | solution.py:13
  157.9 0.0 collective-permute-start.4
  157.9 0.7 iota_compare_fusion.3
  158.6 0.7 fusion.20
  159.3 1.0 fusion.8
  160.3 21.8 %collective-permute-done.4 = bf16[8,64,1024]{2,1,0:T(8,128)(2,1)} collective-permute-done((bf16[8,64,1024]{2,1,0:T(8,128)(2,1)}, bf16[8,64,1024]{2,1,0:T(8,128)(2,1)}, u32[]{:S(2)}, u32[]{:S(2)}) %collective-permute-start.4) | collective-permute-done | bytes 1048608 | tf_op jit(solution)/shard_map/ppermute | solution.py:13
  182.1 1.3 constant_dynamic-update-slice_fusion.4
  183.5 1.3 constant_dynamic-update-slice_fusion.3
  184.8 0.1 constant_dynamic-update-slice_fusion.2
  184.9 0.1 constant_dynamic-update-slice_fusion.1
  185.0 0.0 copy-start
  185.0 0.0 copy-start.1
  185.0 0.1 constant_dynamic-update-slice_fusion
  185.1 6.2 %fusion = bf16[8,2,64,1024]{3,0,2,1:T(8,128)(2,1)S(1)} fusion(bf16[40,64,1024,1]{2,1,0,3:T(8,128)(2,1)S(1)} %bitcast.11, bf16[8,2,40,1]{2,1,0,3:T(2,128)(2,1)S(1)} %fusion.8), kind=kOutput, calls=%fused_computation.1 | convolution fusion | flops 83886080 | bytes 7341312 | tf_op jit(solution)/shard_map/ltp,pmb->ltmb/dot_general | solution.py:48
  191.2 0.0 copy-done
  191.2 0.0 copy-done.1
  191.3 2.9 %fusion.5 = f32[8,1024]{1,0:T(8,128)S(1)} fusion(bf16[8,64,1024]{2,1,0:T(8,128)(2,1)S(1)} %copy-done, bf16[2,1024,1024]{2,1,0:T(8,128)(2,1)S(1)} %copy-done.1, bf16[8,2,64,1024]{3,0,2,1:T(8,128)(2,1)S(1)} %fusion), kind=kOutput, calls=%fused_computation.9 | convolution fusion | flops 2149048320 | bytes 7372800 | tf_op jit(solution)/shard_map/dot_general | solution.py:51
  194.2 0.6 broadcast_multiply_fusion
  194.8 0.0 reduce-scatter.2.cloned.1.call-update
  194.8 16.9 %reduce-scatter.2.cloned.1.call-done = f32[8,256]{1,0:T(8,128)} async-done(((f32[8,1024]{1,0:T(8,128)}), f32[8,256]{1,0:T(8,128)}) %reduce-scatter.2.cloned.1.call-update) | async-done | bytes 8208 | tf_op jit(solution)/shard_map/reduce_scatter | solution.py:55
  (1 shorter events, 0.0 us)
Async XLA Ops:
  6.5 205.2 %reduce-scatter.2.cloned.1.call-start = ((), (), s32[]{:S(2)}) async-start(), calls=%async_computation.1 | async-start | bytes 40960 | tf_op jit(solution)/shard_map/reduce_scatter | solution.py:55
  52.2 27.5 %collective-permute-start = (bf16[8,64,1024]{2,1,0:T(8,128)(2,1)S(1)}, bf16[8,64,1024]{2,1,0:T(8,128)(2,1)S(1)}, u32[]{:S(2)}, u32[]{:S(2)}) collective-permute-start(bf16[8,64,1024]{2,1,0:T(8,128)(2,1)S(1)} %fusion.4), channel_id=1, source_target_pairs={{0,24},{4,28},{8,0},{12,4},{16,8},{20,12},{24,16},{28,20},{1,25},{... | collective-permute-start | bytes 3145736 | tf_op jit(solution)/shard_map/ppermute | solution.py:13
  79.8 27.5 %collective-permute-start.1 = (bf16[8,64,1024]{2,1,0:T(8,128)(2,1)S(1)}, bf16[8,64,1024]{2,1,0:T(8,128)(2,1)S(1)}, u32[]{:S(2)}, u32[]{:S(2)}) collective-permute-start(bf16[8,64,1024]{2,1,0:T(8,128)(2,1)S(1)} %collective-permute-done), channel_id=1, source_target_pairs={{0,4},{4,8},{8,12},{12,16},{16,20},{20,24},{24,28},{28,0},{1,5},{5... | collective-permute-start | bytes 3145736 | tf_op jit(solution)/shard_map/ppermute | solution.py:13
  107.3 25.7 %collective-permute-start.2 = (bf16[8,64,1024]{2,1,0:T(8,128)(2,1)S(1)}, bf16[8,64,1024]{2,1,0:T(8,128)(2,1)S(1)}, u32[]{:S(2)}, u32[]{:S(2)}) collective-permute-start(bf16[8,64,1024]{2,1,0:T(8,128)(2,1)S(1)} %collective-permute-done.1), channel_id=1, source_target_pairs={{0,4},{4,8},{8,12},{12,16},{16,20},{20,24},{24,28},{28,0},{1,5},{5... | collective-permute-start | bytes 3145736 | tf_op jit(solution)/shard_map/ppermute | solution.py:13
  133.0 24.9 %collective-permute-start.3 = (bf16[8,64,1024]{2,1,0:T(8,128)(2,1)S(1)}, bf16[8,64,1024]{2,1,0:T(8,128)(2,1)}, u32[]{:S(2)}, u32[]{:S(2)}) collective-permute-start(bf16[8,64,1024]{2,1,0:T(8,128)(2,1)S(1)} %collective-permute-done.2), channel_id=1, source_target_pairs={{0,4},{4,8},{8,12},{12,16},{16,20},{20,24},{24,28},{28,0},{1,5},{5... | collective-permute-start | bytes 3145736 | tf_op jit(solution)/shard_map/ppermute | solution.py:13
  157.9 24.3 %collective-permute-start.4 = (bf16[8,64,1024]{2,1,0:T(8,128)(2,1)}, bf16[8,64,1024]{2,1,0:T(8,128)(2,1)}, u32[]{:S(2)}, u32[]{:S(2)}) collective-permute-start(bf16[8,64,1024]{2,1,0:T(8,128)(2,1)} %collective-permute-done.3), channel_id=1, source_target_pairs={{0,4},{4,8},{8,12},{12,16},{16,20},{20,24},{24,28},{28,0},{1,5},{5... | collective-permute-start | bytes 3145736 | tf_op jit(solution)/shard_map/ppermute | solution.py:13
  185.0 6.3 %copy-start = (bf16[8,64,1024]{2,1,0:T(8,128)(2,1)S(1)}, bf16[8,64,1024]{2,1,0:T(8,128)(2,1)}, u32[]{:S(2)}) copy-start(bf16[8,64,1024]{2,1,0:T(8,128)(2,1)} %param.7) | copy-start | bytes 3145732
  185.0 6.3 %copy-start.1 = (bf16[2,1024,1024]{2,1,0:T(8,128)(2,1)S(1)}, bf16[2,1024,1024]{2,1,0:T(8,128)(2,1)}, u32[]{:S(2)}) copy-start(bf16[2,1024,1024]{2,1,0:T(8,128)(2,1)} %param.8) | copy-start | bytes 12582916
Sparse Core Ops, SparseCore 0:
  195.0 16.7 reduce-scatter.1
where the time goes:
time: 219 us
  waiting for transfers between devices  137 us (63%)
  other arithmetic  47.7 us (22%)
  between operations  13.5 us (6%)
  matrix products  10.1 us (5%)
  starting transfers between devices  7.16 us (3%)
  local copies, waits for them, and re-layouts  2.89 us (1%)
    ppermute x5, waiting for transfers between devices, from_behind(): lax.ppermute(value, axis, [(i, (i + by) % size) for i in range(size)])  120 us
    scatter-add x1, other arithmetic, on_device(): jnp.zeros((local_blocks * block_width,), jnp.float32).at[obs_cell]  43.4 us
    reduce_scatter x1, waiting for transfers between devices, on_device(): lax.psum_scatter(partial_value, 'member', scatter_dimension=1, tiled=True)  16.9 us
    ppermute x5, starting transfers between devices, from_behind(): lax.ppermute(value, axis, [(i, (i + by) % size) for i in range(size)])  7.16 us
    dot_general x1, matrix products, on_device(): jnp.einsum('ltp,pmb->ltmb', slot_counts, panels, preferred_element_type=j...  6.18 us
  transfers between devices with their start and end apart: 6, of which 6 were waited for; matrix products, arithmetic and copies ran while one was open for 1% of the time, Pallas kernels for 0%

commit v1 on v0

v1 whole, which is shorter than its diff:
```python
import functools

import jax
import jax.numpy as jnp
from jax import lax
from jax.experimental import pallas as pl
from jax.experimental.pallas import tpu as pltpu
from jax.sharding import PartitionSpec as P

M = 256
HOPS = 2
KT = 2
LANES = 128
MC = 16
PIECES = 2
MESH = pl.DeviceIdType.MESH


def kernel(
    states, members, slots,
    tab0, tabs, cells, values, anom, tapers, out,
    av, tv, r1, r2, tab_in, idx, innov, innov_in, hot, low, z, own_w, wr, acc, part, got,
    tab_s, tab_r, idx_s, av_s, tv_s, s1, q1, s2, q2, in_s, in_r, ps, pr,
):
    blocks, mem, width = anom.shape
    chunks = mem // MC
    half = blocks // PIECES
    groups = width // LANES
    cols = width // members
    zero_panel = KT * 3 * blocks
    d = lax.axis_index("state")
    me = lax.axis_index("member")
    even = d % 2 == 0

    def at(ds, dm):
        return ((d + ds + states) % states, (me + dm) % members)

    barrier = pltpu.get_barrier_semaphore()
    count = 0
    for ds in range(-HOPS, HOPS + 1):
        for dm in range(members):
            if ds or dm:
                pl.semaphore_signal(barrier, inc=1, device_id=at(ds, dm), device_id_type=MESH)
                count += 1

    load_a = pltpu.make_async_copy(anom, av, av_s)
    load_t = pltpu.make_async_copy(tapers, tv, tv_s)
    load_a.start()
    load_t.start()
    pl.semaphore_wait(barrier, count)

    def remote(src, dst, send, recv, target):
        return pltpu.make_async_remote_copy(
            src_ref=src, dst_ref=dst, send_sem=send, recv_sem=recv,
            device_id=target, device_id_type=MESH,
        )

    def piece(ref, c, h):
        return ref.at[pl.ds(h * half, half), pl.ds(pl.multiple_of(c * MC, MC), MC), :]

    def send2(c, h):
        return remote(piece(anom, c, h), piece(r2, c, h), s2.at[c, h], q2.at[c, h], at(2, 0))

    def send1(c, h):
        return remote(piece(anom, c, h), piece(r1, c, h), s1.at[c, h], q1.at[c, h], at(1, 0))

    def relay(c, h):
        return remote(piece(r2, c, h), piece(r1, c, h), s1.at[c, h], q1.at[c, h], at(-1, 0))

    def send_tab(u):
        return remote(tabs.at[u - 1], tab_in.at[u - 1], tab_s.at[u - 1], tab_r.at[u - 1], at(u, 0))

    def send_innov(u):
        return remote(innov, innov_in.at[u - 1], in_s.at[u - 1], in_r.at[u - 1], at(u, 0))

    def send_part(u, k):
        return remote(
            part.at[u, (me + k) % members], got.at[u, k], ps.at[u, k], pr.at[u, k], at(-u, k)
        )

    for u in (1, 2):
        send_tab(u).start()
    for h in range(PIECES):
        send2(0, h).start()

    @pl.when(even)
    def _():
        for h in range(PIECES):
            send1(0, h).start()

    acc[...] = jnp.zeros_like(acc)

    def hot_row(k, carry):
        cell = cells[pl.ds(k, 1), :]
        value = values[pl.ds(k, 1), :]
        lo = cell & (LANES - 1)
        block = cell // width
        group = (cell // LANES) % groups
        hi = group * blocks + block
        v1 = value.astype(jnp.bfloat16).astype(jnp.float32)
        rest = value - v1
        v2 = rest.astype(jnp.bfloat16).astype(jnp.float32)
        v3 = rest - v2
        rows = blocks * groups
        same = lax.broadcasted_iota(jnp.int32, (rows, LANES), 0) == hi
        where = pl.ds(pl.multiple_of(k * LANES, LANES), LANES)
        for n, v in enumerate((v1, v2, v3)):
            hot[pl.ds(n * rows, rows), where] = jnp.where(
                same, jnp.broadcast_to(v, (rows, LANES)), 0.0
            ).astype(jnp.bfloat16)
        low[:, where] = jnp.where(
            lax.broadcasted_iota(jnp.int32, (LANES, LANES), 0) == lo, 1.0, 0.0
        ).astype(jnp.bfloat16)
        return carry

    lax.fori_loop(0, cells.shape[0], hot_row, 0)
    rows = blocks * groups
    sums = lax.dot_general(
        hot[...], low[...], (((1,), (1,)), ((), ())), preferred_element_type=jnp.float32
    )
    total = sums[0:rows] + sums[rows : 2 * rows] + sums[2 * rows : 3 * rows]
    for g in range(groups):
        innov[:, g * LANES : (g + 1) * LANES] = total[g * blocks : (g + 1) * blocks]
    for u in (1, 2):
        send_innov(u).start()

    def rest_of(c, carry):
        for h in range(PIECES):
            send2(c, h).start()

        @pl.when(even)
        def _():
            for h in range(PIECES):
                send1(c, h).start()

        return carry

    lax.fori_loop(1, chunks, rest_of, 0)

    load_a.wait()
    for j in range(blocks):
        own_w[:, j] = (
            av[j].astype(jnp.float32) * innov[pl.ds(j, 1), :]
        ).astype(jnp.bfloat16).reshape(chunks, MC, width)
    load_t.wait()
    nw = width // 2

    def own_z(n, carry):
        c, t, x = n // (2 * KT), (n // 2) % KT, n % 2
        where = pl.ds(pl.multiple_of(x * nw, nw), nw)
        res = lax.dot_general(
            own_w[c].reshape(blocks * MC, width), tv[t, where, :],
            (((1,), (1,)), ((), ())), preferred_element_type=jnp.float32,
        )
        z[c, pl.ds(t * 3 * blocks, blocks), :, where] = res.reshape(blocks, MC, nw)
        return carry

    lax.fori_loop(0, chunks * KT * 2, own_z, 0)
    for c in range(chunks):
        z[c, zero_panel] = jnp.zeros((MC, width), jnp.float32)

    for u in (1, 2):
        send_tab(u).wait_recv()
        fill = pltpu.make_async_copy(tab_in.at[u - 1], idx.at[u - 1], idx_s.at[u - 1])
        fill.start()
        fill.wait()

    def pairs(c, u, table, source):
        def one(i, carry):
            total = z[c, table(i, 0)]
            for s in range(1, slots):
                total = total + z[c, table(i, s)]
            value = source[i, pl.ds(pl.multiple_of(c * MC, MC), MC), :].astype(jnp.float32) * total
            acc[u, i] += jnp.sum(value.reshape(MC // 8, 8, width), axis=0)
            return carry

        lax.fori_loop(0, blocks, one, 0)

    def fold(u):
        for i in range(blocks):
            row = jnp.sum(acc[u, i], axis=0, keepdims=True)
            for m in range(members):
                part[u, m, i : i + 1, :] = row[:, m * cols : (m + 1) * cols]

    def step(c, carry):
        for h in range(PIECES):
            send2(c, h).wait_recv()

            @pl.when(jnp.logical_not(even))
            def _():
                relay(c, h).start()

        pairs(c, 2, lambda i, s: idx[1, i, s], r2)
        for h in range(PIECES):
            send1(c, h).wait_recv()
        pairs(c, 1, lambda i, s: idx[0, i, s], r1)

        @pl.when(c == 0)
        def _():
            for u in (1, 2):
                send_innov(u).wait_recv()

        @pl.when(c == chunks - 1)
        def _():
            for u in (2, 1):
                fold(u)
                for k in range(members):
                    send_part(u, k).start()

        for g, r in enumerate((r1, r2)):
            for j in range(blocks):
                wr[g * blocks + j] = (
                    r[j, pl.ds(pl.multiple_of(c * MC, MC), MC), :].astype(jnp.float32)
                    * innov_in[g, pl.ds(j, 1), :]
                ).astype(jnp.bfloat16)

        def far_z(n, carry):
            t, x = n // 2, n % 2
            where = pl.ds(pl.multiple_of(x * nw, nw), nw)
            res = lax.dot_general(
                wr[...].reshape(2 * blocks * MC, width), tv[t, where, :],
                (((1,), (1,)), ((), ())), preferred_element_type=jnp.float32,
            )
            z[c, pl.ds(t * 3 * blocks + blocks, 2 * blocks), :, where] = res.reshape(
                2 * blocks, MC, nw
            )
            return carry

        lax.fori_loop(0, KT * 2, far_z, 0)
        pairs(c, 0, lambda i, s: tab0[i, s], av)
        return carry

    lax.fori_loop(0, chunks, step, 0)
    fold(0)
    for k in range(1, members):
        send_part(0, k).start()
    total = part[0, me]
    for u in (2, 1, 0):
        for k in range(members):
            if u or k:
                send_part(u, k).wait_recv()
                total = total + got[u, k]
    out[...] = total / jnp.float32(M - 1)

    for u in (0, 1, 2):
        for k in range(members):
            if u or k:
                send_part(u, k).wait_send()
    for u in (1, 2):
        send_tab(u).wait_send()
        send_innov(u).wait_send()

    def drain(c, carry):
        for h in range(PIECES):
            send2(c, h).wait_send()
            send1(c, h).wait_send()
        return carry

    lax.fori_loop(0, chunks, drain, 0)


def on_device(states, members, anomalies, tapers, nbr_block, taper_index, pair_count, obs_cell, obs_value):
    blocks, mem, width = anomalies.shape
    slots = nbr_block.shape[1]
    chunks = mem // MC
    cols = width // members
    d = lax.axis_index("state")
    gap = (nbr_block // blocks - d + HOPS + states) % states - HOPS
    valid = jnp.arange(slots, dtype=jnp.int32)[None, :] < pair_count[:, None]
    base = taper_index * (3 * blocks) + nbr_block % blocks
    none = KT * 3 * blocks
    tab0 = jnp.where(valid & (gap <= 0), base - gap * blocks, none)
    tabs = jnp.stack([jnp.where(valid & (gap == u), base, none) for u in (1, 2)])
    tabs = jnp.pad(tabs, ((0, 0), (0, 0), (0, LANES - slots)))
    cells = obs_cell.reshape(-1, LANES)
    values = obs_value.reshape(-1, LANES)
    rows = blocks * (width // LANES)
    dma = pltpu.SemaphoreType.DMA
    any_space = pl.BlockSpec(memory_space=pl.ANY)
    vmem = pl.BlockSpec(memory_space=pltpu.VMEM)
    return pl.pallas_call(
        functools.partial(kernel, states, members, slots),
        out_shape=jax.ShapeDtypeStruct((blocks, cols), jnp.float32),
        in_specs=[pl.BlockSpec(memory_space=pltpu.SMEM), any_space, vmem, vmem, any_space, any_space],
        out_specs=vmem,
        scratch_shapes=[
            pltpu.VMEM((blocks, mem, width), jnp.bfloat16),
            pltpu.VMEM(tapers.shape, jnp.bfloat16),
            pltpu.VMEM((blocks, mem, width), jnp.bfloat16),
            pltpu.VMEM((blocks, mem, width), jnp.bfloat16),
            pltpu.VMEM((2, blocks, LANES), jnp.int32),
            pltpu.SMEM((2, blocks, LANES), jnp.int32),
            pltpu.VMEM((blocks, width), jnp.float32),
            pltpu.VMEM((2, blocks, width), jnp.float32),
            pltpu.VMEM((3 * rows, obs_cell.shape[0]), jnp.bfloat16),
            pltpu.VMEM((LANES, obs_cell.shape[0]), jnp.bfloat16),
            pltpu.VMEM((chunks, KT * 3 * blocks + 1, MC, width), jnp.float32),
            pltpu.VMEM((chunks, blocks, MC, width), jnp.bfloat16),
            pltpu.VMEM((2 * blocks, MC, width), jnp.bfloat16),
            pltpu.VMEM((3, blocks, 8, width), jnp.float32),
            pltpu.VMEM((3, members, blocks, cols), jnp.float32),
            pltpu.VMEM((3, members, blocks, cols), jnp.float32),
            dma((2,)), dma((2,)), dma((2,)), dma, dma,
            dma((chunks, PIECES)), dma((chunks, PIECES)),
            dma((chunks, PIECES)), dma((chunks, PIECES)),
            dma((2,)), dma((2,)),
            dma((3, members)), dma((3, members)),
        ],
        compiler_params=pltpu.CompilerParams(
            collective_id=0, has_side_effects=True, vmem_limit_bytes=48 * 1024 * 1024
        ),
    )(tab0, tabs, cells, values, anomalies, tapers)


def solution(mesh):
    placed = (
        P("state", "member", None),
        P(),
        P("state", None),
        P("state", None),
        P("state"),
        P("state"),
        P("state"),
    )
    return jax.shard_map(
        functools.partial(on_device, mesh.shape["state"], mesh.shape["member"]),
        mesh=mesh, in_specs=placed, out_specs=P("state", "member"), check_vma=False,
    )
```

time: 219 us -> 57.4 us (0.26)
  waiting for transfers between devices: 137 us -> 0 us
  Pallas kernels: 0 us -> 50.7 us
  other arithmetic: 47.7 us -> 0.8 us
  between operations: 13.5 us -> 0.02 us
  matrix products: 10.1 us -> 0 us
  starting transfers between devices: 7.16 us -> 0 us
  local copies, waits for them, and re-layouts: 2.89 us -> 5.53 us
    ppermute x5 -> x0, waiting for transfers between devices: 120 us -> none  [from_behind(): lax.ppermute(value, axis, [(i, (i + by) % size) for i in range(size)])]
    pallas_call x0 -> x1, Pallas kernels: none -> 50.7 us  [on_device(): pl.pallas_call(functools.partial(kernel, states, members, slots), out_sha...]
    scatter-add x1 -> x0, other arithmetic: 43.4 us -> none  [on_device(): jnp.zeros((local_blocks * block_width,), jnp.float32).at[obs_cell]]
    reduce_scatter x1 -> x0, waiting for transfers between devices: 16.9 us -> none  [on_device(): lax.psum_scatter(partial_value, 'member', scatter_dimension=1, tiled=True)]
    dot_general x3 -> x0, matrix products: 10.1 us -> none  [the longest x1 6.18 us: on_device(): jnp.einsum('ltp,pmb->ltmb', slot_counts, panels, preferred_element_type=j...]
    ppermute x5 -> x0, starting transfers between devices: 7.16 us -> none  [from_behind(): lax.ppermute(value, axis, [(i, (i + by) % size) for i in range(size)])]
    unnamed x8 -> x9, local copies, waits for them, and re-layouts: 2.81 us -> 5.52 us
  transfers between devices with their start and end apart: 6 -> 0, of which waited for: 6 -> 0; matrix products, arithmetic and copies ran while one was open for 1% -> 0% of each run, Pallas kernels for 0% -> 0%
where the time goes in v1:
time: 57.4 us; the launch traced here: 57 us
  Pallas kernels  50.7 us (88%)
  local copies, waits for them, and re-layouts  5.53 us (10%)
  other arithmetic  0.8 us (1%)
    pallas_call x1, Pallas kernels, on_device(): pl.pallas_call(functools.partial(kernel, states, members, slots), out_sha...  50.7 us
    unnamed x9, local copies, waits for them, and re-layouts  5.52 us

profile of v1, /device:TPU:0, one launch (start us, length us, event | category | flops | bytes accessed | tf_op | source)
XLA Modules:
  0.0 57.0 jit_solution(5895719764938976312)
XLA Ops:
  0.0 0.8 %select_bitcast_fusion.1 = (s32[1,8,12]{2,1,0:T(8,128)S(1)}, s32[1,8,12]{2,1,0:T(8,128)S(1)}, s32[8,12]{1,0:T(8,128)S(1)}) fusion(s32[8]{0:T(128)} %param.11, s32[8,12]{1,0:T(8,128)} %param.9, s32[8,12]{1,0:T(8,128)} %param.10, s32[]{:T(128)S(6)} %axis_index.15), kind=kLoop, calls=%fused_computation.15 | loop fusion | flops 4512 | bytes 1956 | tf_op jit(solution)/shard_map/stack | solution.py:273
  0.8 0.0 copy-start
  0.8 2.2 %copy-done = bf16[2,1024,1024]{2,1,0:T(8,128)(2,1)S(1)} copy-done((bf16[2,1024,1024]{2,1,0:T(8,128)(2,1)S(1)}, bf16[2,1024,1024]{2,1,0:T(8,128)(2,1)}, u32[]{:S(2)}) %copy-start) | copy-done | bytes 4194328
  3.0 0.0 copy-start.1
  3.0 1.2 %copy-done.1 = bf16[8,64,1024]{2,1,0:T(8,128)(2,1)S(1)} copy-done((bf16[8,64,1024]{2,1,0:T(8,128)(2,1)S(1)}, bf16[8,64,1024]{2,1,0:T(8,128)(2,1)}, u32[]{:S(2)}) %copy-start.1) | copy-done | bytes 1048600
  4.2 0.0 copy-start.2
  4.2 0.8 %copy-done.2 = s32[8192]{0:T(1024)S(1)} copy-done((s32[8192]{0:T(1024)S(1)}, s32[8192]{0:T(1024)}, u32[]{:S(2)}) %copy-start.2) | copy-done | bytes 32792
  5.0 0.0 copy-start.3
  5.0 0.8 %copy-done.3 = f32[8192]{0:T(1024)S(1)} copy-done((f32[8192]{0:T(1024)S(1)}, f32[8192]{0:T(1024)}, u32[]{:S(2)}) %copy-start.3) | copy-done | bytes 32792
  5.7 50.7 %shard_map.73 = f32[8,256]{1,0:T(8,128)S(1)} custom-call(s32[8,12]{1,0:T(8,128)S(1)} %get-tuple-element.7.tab0, s32[2,8,128]{2,1,0:T(8,128)S(1)} %pad.4.tabs, s32[64,128]{1,0:T(8,128)S(1)} %bitcast.6, f32[64,128]{1,0:T(8,128)S(1)} %bitcast.7, bf16[8,64,1024]{2,1,0:T(8,128)(2,1)S(1)} %copy-done.1, bf16[2,1024,1024]{2,1,0:T(8,128)(2,1)S(1)} %copy-done), custom_call_target="tpu_custom_call" | custom-call | tf_op jit(solution)/shard_map/pallas_call | solution.py:281
  56.4 0.6 %copy.9 = f32[8,256]{1,0:T(8,128)} copy(f32[8,256]{1,0:T(8,128)S(1)} %shard_map.73) | data formatting | bytes 16384
  (2 shorter events, 0.0 us)
Async XLA Ops:
  0.8 2.2 %copy-start = (bf16[2,1024,1024]{2,1,0:T(8,128)(2,1)S(1)}, bf16[2,1024,1024]{2,1,0:T(8,128)(2,1)}, u32[]{:S(2)}) copy-start(bf16[2,1024,1024]{2,1,0:T(8,128)(2,1)} %tapers.1) | copy-start | bytes 12582916
  3.0 1.2 %copy-start.1 = (bf16[8,64,1024]{2,1,0:T(8,128)(2,1)S(1)}, bf16[8,64,1024]{2,1,0:T(8,128)(2,1)}, u32[]{:S(2)}) copy-start(bf16[8,64,1024]{2,1,0:T(8,128)(2,1)} %anom.1) | copy-start | bytes 3145732
  4.2 0.8 %copy-start.2 = (s32[8192]{0:T(1024)S(1)}, s32[8192]{0:T(1024)}, u32[]{:S(2)}) copy-start(s32[8192]{0:T(1024)} %param.12) | copy-start | bytes 98308
  5.0 0.8 %copy-start.3 = (f32[8192]{0:T(1024)S(1)}, f32[8192]{0:T(1024)}, u32[]{:S(2)}) copy-start(f32[8192]{0:T(1024)} %param.13) | copy-start | bytes 98308

commit v2 on v1

v2 whole, which is shorter than its diff:
```python
import functools

import jax
import jax.numpy as jnp
from jax import lax
from jax.experimental import pallas as pl
from jax.experimental.pallas import tpu as pltpu
from jax.sharding import PartitionSpec as P

M = 256
HOPS = 2
KT = 2
LANES = 128
MC = 16
PIECES = 1
MESH = pl.DeviceIdType.MESH


def kernel(
    states, members, slots,
    tab0_hbm, tabs, cells_hbm, values_hbm, anom, tapers, out,
    tab0, cells, values, obs_s, av, tv, r1, r2, tab_in, idx, innov, innov_in, hot, low, z, own_w, wr, acc, part, got,
    tab_s, tab_r, idx_s, av_s, tv_s, s1, q1, s2, q2, in_s, in_r, ps, pr, peers,
):
    blocks, mem, width = anom.shape
    chunks = mem // MC
    half = blocks // PIECES
    groups = width // LANES
    cols = width // members
    zero_panel = KT * 3 * blocks
    d = lax.axis_index("state")
    me = lax.axis_index("member")
    odd = d % 2
    sign = 1 - 2 * odd
    heavy = chunks // 2

    def at(ds, dm):
        return ((d + ds + states) % states, (me + dm) % members)

    barrier = pltpu.get_barrier_semaphore()
    greeted = [(sign, 0), (2, 0), (-2, 0)] + [(0, k) for k in range(1, members)]
    for ds, dm in greeted:
        pl.semaphore_signal(barrier, inc=1, device_id=at(ds, dm), device_id_type=MESH)

    load_a = pltpu.make_async_copy(anom, av, av_s)
    load_t = pltpu.make_async_copy(tapers, tv, tv_s)
    load_c = pltpu.make_async_copy(cells_hbm, cells, obs_s.at[0])
    load_v = pltpu.make_async_copy(values_hbm, values, obs_s.at[1])
    load_i = pltpu.make_async_copy(tab0_hbm, tab0, obs_s.at[2])
    for load in (load_c, load_v, load_i, load_a, load_t):
        load.start()

    def remote(src, dst, send, recv, target):
        return pltpu.make_async_remote_copy(
            src_ref=src, dst_ref=dst, send_sem=send, recv_sem=recv,
            device_id=target, device_id_type=MESH,
        )

    def members_of(c, shift):
        return pl.ds(pl.multiple_of(((c + shift * heavy) % chunks) * MC, MC), MC)

    def piece(ref, c, h, shift):
        return ref.at[pl.ds(h * half, half), members_of(c, shift), :]

    def send2(c, h):
        return remote(
            piece(anom, c, h, odd), piece(r2, c, h, 0), s2.at[c, h], q2.at[c, h], at(-2 * sign, 0)
        )

    def send1(c):
        return remote(
            anom.at[:, members_of(c, 1 - odd), :], r1.at[:, members_of(c, 0), :],
            s1.at[c], q1.at[c], at(sign, 0),
        )

    def to(u):
        return sign if u == 1 else -2 * sign

    def send_tab(u):
        return remote(tabs.at[u - 1], tab_in.at[u - 1], tab_s.at[u - 1], tab_r.at[u - 1], at(to(u), 0))

    def send_innov(u):
        return remote(innov, innov_in.at[u - 1], in_s.at[u - 1], in_r.at[u - 1], at(to(u), 0))

    def send_part(u, k):
        return remote(
            part.at[u, (me + k) % members], got.at[u, k], ps.at[u, k], pr.at[u, k],
            at((0, sign, 2 * sign)[u], k),
        )

    acc[...] = jnp.zeros_like(acc)

    def hot_row(k, carry):
        cell = cells[pl.ds(k, 1), :]
        value = values[pl.ds(k, 1), :]
        lo = cell & (LANES - 1)
        block = cell // width
        group = (cell // LANES) % groups
        hi = group * blocks + block
        v1 = value.astype(jnp.bfloat16).astype(jnp.float32)
        rest = value - v1
        v2 = rest.astype(jnp.bfloat16).astype(jnp.float32)
        v3 = rest - v2
        rows = blocks * groups
        same = lax.broadcasted_iota(jnp.int32, (rows, LANES), 0) == hi
        where = pl.ds(pl.multiple_of(k * LANES, LANES), LANES)
        for n, v in enumerate((v1, v2, v3)):
            hot[pl.ds(n * rows, rows), where] = jnp.where(
                same, jnp.broadcast_to(v, (rows, LANES)), 0.0
            ).astype(jnp.bfloat16)
        low[:, where] = jnp.where(
            lax.broadcasted_iota(jnp.int32, (LANES, LANES), 0) == lo, 1.0, 0.0
        ).astype(jnp.bfloat16)
        return carry

    load_c.wait()
    load_v.wait()
    load_i.wait()
    lax.fori_loop(0, cells.shape[0], hot_row, 0)
    rows = blocks * groups
    sums = lax.dot_general(
        hot[...], low[...], (((1,), (1,)), ((), ())), preferred_element_type=jnp.float32
    )
    total = sums[0:rows] + sums[rows : 2 * rows] + sums[2 * rows : 3 * rows]
    for g in range(groups):
        innov[:, g * LANES : (g + 1) * LANES] = total[g * blocks : (g + 1) * blocks]
    pl.semaphore_wait(barrier, len(greeted))
    for u in (1, 2):
        send_tab(u).start()
        send_innov(u).start()

    def send_all(c, carry):
        for h in range(PIECES):
            send2(c, h).start()
        return carry

    for c in range(heavy):
        send1(c).start()
    lax.fori_loop(0, chunks, send_all, 0)
    for k in range(1, members):
        pl.semaphore_signal(peers, inc=1, device_id=at(0, k), device_id_type=MESH)

    load_a.wait()
    for c in range(chunks):
        for j in range(blocks):
            own_w[c, j] = (
                av[j, members_of(c, odd), :].astype(jnp.float32) * innov[pl.ds(j, 1), :]
            ).astype(jnp.bfloat16)
    load_t.wait()
    nw = width // 4

    def own_z(n, carry):
        t, x = n // 4, n % 4
        where = pl.ds(pl.multiple_of(x * nw, nw), nw)
        res = lax.dot_general(
            own_w[...].reshape(chunks * blocks * MC, width), tv[t, where, :],
            (((1,), (1,)), ((), ())), preferred_element_type=jnp.float32,
        )
        z[:, pl.ds(t * 3 * blocks, blocks), :, where] = res.reshape(chunks, blocks, MC, nw)
        return carry

    lax.fori_loop(0, KT * 4, own_z, 0)
    for c in range(heavy, chunks):
        for t in range(KT):
            z[c, (t * 3 + 1) * blocks : (t * 3 + 2) * blocks] = jnp.zeros((blocks, MC, width), jnp.float32)
    for c in range(chunks):
        z[c, zero_panel] = jnp.zeros((MC, width), jnp.float32)

    for u in (1, 2):
        send_tab(u).wait_recv()
        fill = pltpu.make_async_copy(tab_in.at[u - 1], idx.at[u - 1], idx_s.at[u - 1])
        fill.start()
        fill.wait()

    def pairs(c, u, table, source, shift):
        def one(i, carry):
            total = z[c, table(i, 0)]
            for s in range(1, slots):
                total = total + z[c, table(i, s)]
            value = source[i, members_of(c, shift), :].astype(jnp.float32) * total
            acc[u, i] += jnp.sum(value.reshape(MC // 8, 8, width), axis=0)
            return carry

        lax.fori_loop(0, blocks, one, 0)

    def fold(u):
        for i in range(blocks):
            row = jnp.sum(acc[u, i], axis=0, keepdims=True)
            for m in range(members):
                part[u, m, i : i + 1, :] = row[:, m * cols : (m + 1) * cols]

    def step(full, c, carry):
        for h in range(PIECES):
            send2(c, h).wait_recv()
        if full:
            send1(c).wait_recv()
        else:
            pairs(c, 2, lambda i, s: idx[1, i, s], r2, 0)

            @pl.when(c == chunks - 1)
            def _():
                fold(2)
                for k in range(members):
                    send_part(2, k).start()

        first = 0 if full else blocks
        for g, r in enumerate((r1, r2)):
            if g or full:
                for j in range(blocks):
                    wr[g * blocks + j] = (
                        r[j, members_of(c, 0), :].astype(jnp.float32)
                        * innov_in[g, pl.ds(j, 1), :]
                    ).astype(jnp.bfloat16)
        count = 2 * blocks - first

        def far_z(n, carry):
            t, x = n // 4, n % 4
            where = pl.ds(pl.multiple_of(x * nw, nw), nw)
            res = lax.dot_general(
                wr[pl.ds(first, count)].reshape(count * MC, width), tv[t, where, :],
                (((1,), (1,)), ((), ())), preferred_element_type=jnp.float32,
            )
            z[c, pl.ds(t * 3 * blocks + blocks + first, count), :, where] = res.reshape(
                count, MC, nw
            )
            return carry

        lax.fori_loop(0, KT * 4, far_z, 0)
        if full:
            pairs(c, 2, lambda i, s: idx[1, i, s], r2, 0)
            pairs(c, 1, lambda i, s: idx[0, i, s], r1, 0)
        pairs(c, 0, lambda i, s: tab0[i, s], av, odd)
        return carry

    for u in (1, 2):
        send_innov(u).wait_recv()
    lax.fori_loop(0, heavy, functools.partial(step, True), 0)
    fold(1)
    pl.semaphore_wait(peers, members - 1)
    for k in range(members):
        send_part(1, k).start()
    lax.fori_loop(heavy, chunks, functools.partial(step, False), 0)
    fold(0)
    for k in range(1, members):
        send_part(0, k).start()
    total = part[0, me]
    for u in (2, 1, 0):
        for k in range(members):
            if u or k:
                send_part(u, k).wait_recv()
                total = total + got[u, k]
    out[...] = total / jnp.float32(M - 1)

    for u in (0, 1, 2):
        for k in range(members):
            if u or k:
                send_part(u, k).wait_send()
    for u in (1, 2):
        send_tab(u).wait_send()
        send_innov(u).wait_send()

    def drain(c, carry):
        for h in range(PIECES):
            send2(c, h).wait_send()
        return carry

    lax.fori_loop(0, chunks, drain, 0)
    for c in range(heavy):
        send1(c).wait_send()


def on_device(states, members, anomalies, tapers, nbr_block, taper_index, pair_count, obs_cell, obs_value):
    blocks, mem, width = anomalies.shape
    slots = nbr_block.shape[1]
    chunks = mem // MC
    cols = width // members
    d = lax.axis_index("state")
    gap = (nbr_block // blocks - d + HOPS + states) % states - HOPS
    valid = jnp.arange(slots, dtype=jnp.int32)[None, :] < pair_count[:, None]
    base = taper_index * (3 * blocks) + nbr_block % blocks
    none = KT * 3 * blocks
    sign = 1 - 2 * (d % 2)
    gap = gap * sign
    tab0 = jnp.where(valid & (gap >= 0), base + gap * blocks, none)
    tab0 = jnp.pad(tab0, ((0, 0), (0, LANES - slots)))
    near = jnp.where(gap == 1, base, jnp.where(gap == -1, base + 2 * blocks, none))
    far = jnp.where(gap == -2, base, jnp.where(gap == -1, base + blocks, none))
    tabs = jnp.where(valid, jnp.stack([near, far]), none)
    tabs = jnp.pad(tabs, ((0, 0), (0, 0), (0, LANES - slots)))
    cells = obs_cell.reshape(-1, LANES)
    values = obs_value.reshape(-1, LANES)
    rows = blocks * (width // LANES)
    dma = pltpu.SemaphoreType.DMA
    any_space = pl.BlockSpec(memory_space=pl.ANY)
    vmem = pl.BlockSpec(memory_space=pltpu.VMEM)
    return pl.pallas_call(
        functools.partial(kernel, states, members, slots),
        out_shape=jax.ShapeDtypeStruct((blocks, cols), jnp.float32),
        in_specs=[any_space] * 6,
        out_specs=vmem,
        scratch_shapes=[
            pltpu.SMEM((blocks, LANES), jnp.int32),
            pltpu.VMEM(cells.shape, jnp.int32),
            pltpu.VMEM(values.shape, jnp.float32),
            dma((3,)),
            pltpu.VMEM((blocks, mem, width), jnp.bfloat16),
            pltpu.VMEM(tapers.shape, jnp.bfloat16),
            pltpu.VMEM((blocks, mem, width), jnp.bfloat16),
            pltpu.VMEM((blocks, mem, width), jnp.bfloat16),
            pltpu.VMEM((2, blocks, LANES), jnp.int32),
            pltpu.SMEM((2, blocks, LANES), jnp.int32),
            pltpu.VMEM((blocks, width), jnp.float32),
            pltpu.VMEM((2, blocks, width), jnp.float32),
            pltpu.VMEM((3 * rows, obs_cell.shape[0]), jnp.bfloat16),
            pltpu.VMEM((LANES, obs_cell.shape[0]), jnp.bfloat16),
            pltpu.VMEM((chunks, KT * 3 * blocks + 1, MC, width), jnp.float32),
            pltpu.VMEM((chunks, blocks, MC, width), jnp.bfloat16),
            pltpu.VMEM((2 * blocks, MC, width), jnp.bfloat16),
            pltpu.VMEM((3, blocks, 8, width), jnp.float32),
            pltpu.VMEM((3, members, blocks, cols), jnp.float32),
            pltpu.VMEM((3, members, blocks, cols), jnp.float32),
            dma((2,)), dma((2,)), dma((2,)), dma, dma,
            dma((chunks,)), dma((chunks,)),
            dma((chunks, PIECES)), dma((chunks, PIECES)),
            dma((2,)), dma((2,)),
            dma((3, members)), dma((3, members)),
            pltpu.SemaphoreType.REGULAR,
        ],
        compiler_params=pltpu.CompilerParams(
            collective_id=0, has_side_effects=True, vmem_limit_bytes=67_043_328
        ),
    )(tab0, tabs, cells, values, anomalies, tapers)


def solution(mesh):
    placed = (
        P("state", "member", None),
        P(),
        P("state", None),
        P("state", None),
        P("state"),
        P("state"),
        P("state"),
    )
    return jax.shard_map(
        functools.partial(on_device, mesh.shape["state"], mesh.shape["member"]),
        mesh=mesh, in_specs=placed, out_specs=P("state", "member"), check_vma=False,
    )
```

time: 57.4 us -> 44 us (0.77)
  the two profiles are of different devices: /device:TPU:0 before, /device:TPU:5 now
where the time goes in v2:
time: 44 us; the launch traced here: 43.8 us
  Pallas kernels  39.8 us (90%)
  local copies, waits for them, and re-layouts  2.49 us (6%)
  other arithmetic  1.51 us (3%)
    pallas_call x1, Pallas kernels, on_device(): pl.pallas_call(functools.partial(kernel, states, members, slots), out_sha...  39.8 us
    unnamed x1, local copies, waits for them, and re-layouts  1.3 us

profile of v2, /device:TPU:5, one launch (start us, length us, event | category | flops | bytes accessed | tf_op | source)
XLA Modules:
  0.0 43.8 jit_solution(4506461496450331513)
XLA Ops:
  0.0 0.7 %iota_compare_fusion = pred[8,12]{1,0:T(8,128)(4,1)S(1)} fusion(s32[8]{0:T(128)} %param.11), kind=kLoop, calls=%fused_computation.19 | loop fusion | flops 96 | bytes 128 | tf_op jit(solution)/shard_map/lt | solution.py:279
  0.7 0.8 %select_bitcast_fusion.1 = (s32[1,8,12]{2,1,0:T(8,128)S(1)}, s32[8,12]{1,0:T(8,128)S(1)}, s32[1,8,12]{2,1,0:T(8,128)S(1)}) fusion(s32[8,12]{1,0:T(8,128)} %param.9, s32[8,12]{1,0:T(8,128)} %param.10, s32[]{:T(128)S(6)} %sub.22, s32[]{:T(128)S(6)} %axis_index.15, s32[8]{0:T(128)} %param.11), kind=kLoop, calls=%fused_computation.16 | loop fusion | flops 4896 | bytes 1960 | tf_op jit(solution)/shard_map/stack | solution.py:288
  1.5 0.6 %pad.9.tabs = s32[2,8,128]{2,1,0:T(8,128)} pad(s32[2,8,12]{2,1,0:T(8,128)S(1)} %add_select_fusion, s32[]{:T(128)} %constant.55.clone.1), padding=0_0x0_0x0_116 | pad | bytes 8964 | tf_op jit(solution)/shard_map/jit(_pad)/pad | solution.py:289
  2.1 0.6 %pad.8.tab0_hbm = s32[8,128]{1,0:T(8,128)} pad(s32[8,12]{1,0:T(8,128)S(1)} %get-tuple-element.6, s32[]{:T(128)} %constant.55.clone.1), padding=0_0x0_116 | pad | bytes 4484 | tf_op jit(solution)/shard_map/jit(_pad)/pad | solution.py:285
  2.7 39.8 %shard_map.73 = f32[8,256]{1,0:T(8,128)} custom-call(s32[8,128]{1,0:T(8,128)} %pad.8.tab0_hbm, s32[2,8,128]{2,1,0:T(8,128)} %pad.9.tabs, s32[64,128]{1,0:T(8,128)} %bitcast.6, f32[64,128]{1,0:T(8,128)} %bitcast.7, bf16[8,64,1024]{2,1,0:T(8,128)(2,1)} %anom.1, bf16[2,1024,1024]{2,1,0:T(8,128)(2,1)} %tapers.1), custom_call_target="tpu_custom_call" | custom-call | tf_op jit(solution)/shard_map/pallas_call | solution.py:296
  42.5 1.3 %copy.9 = f32[8,256]{1,0:T(8,128)} copy(f32[8,256]{1,0:T(8,128)} %shard_map.73) | data formatting | bytes 16384
  (1 shorter events, 0.0 us)

commit v3 on v2

--- a/solution.py
+++ b/solution.py
@@ -88,6 +88,12 @@
             at((0, sign, 2 * sign)[u], k),
         )
 
+    pl.semaphore_wait(barrier, len(greeted))
+    for u in (1, 2):
+        send_tab(u).start()
+    for h in range(PIECES):
+        send2(0, h).start()
+    send1(0).start()
     acc[...] = jnp.zeros_like(acc)
 
     def hot_row(k, carry):
@@ -124,9 +130,7 @@
     total = sums[0:rows] + sums[rows : 2 * rows] + sums[2 * rows : 3 * rows]
     for g in range(groups):
         innov[:, g * LANES : (g + 1) * LANES] = total[g * blocks : (g + 1) * blocks]
-    pl.semaphore_wait(barrier, len(greeted))
-    for u in (1, 2):
-        send_tab(u).start()
+    for u in (1, 2):
         send_innov(u).start()
 
     def send_all(c, carry):
@@ -134,9 +138,9 @@
             send2(c, h).start()
         return carry
 
-    for c in range(heavy):
+    for c in range(1, heavy):
         send1(c).start()
-    lax.fori_loop(0, chunks, send_all, 0)
+    lax.fori_loop(1, chunks, send_all, 0)
     for k in range(1, members):
         pl.semaphore_signal(peers, inc=1, device_id=at(0, k), device_id_type=MESH)
 
@@ -147,10 +151,10 @@
                 av[j, members_of(c, odd), :].astype(jnp.float32) * innov[pl.ds(j, 1), :]
             ).astype(jnp.bfloat16)
     load_t.wait()
-    nw = width // 4
+    nw = width // 2
 
     def own_z(n, carry):
-        t, x = n // 4, n % 4
+        t, x = n // 2, n % 2
         where = pl.ds(pl.multiple_of(x * nw, nw), nw)
         res = lax.dot_general(
             own_w[...].reshape(chunks * blocks * MC, width), tv[t, where, :],
@@ -159,7 +163,7 @@
         z[:, pl.ds(t * 3 * blocks, blocks), :, where] = res.reshape(chunks, blocks, MC, nw)
         return carry
 
-    lax.fori_loop(0, KT * 4, own_z, 0)
+    lax.fori_loop(0, KT * 2, own_z, 0)
     for c in range(heavy, chunks):
         for t in range(KT):
             z[c, (t * 3 + 1) * blocks : (t * 3 + 2) * blocks] = jnp.zeros((blocks, MC, width), jnp.float32)
@@ -214,7 +218,7 @@
         count = 2 * blocks - first
 
         def far_z(n, carry):
-            t, x = n // 4, n % 4
+            t, x = n // 2, n % 2
             where = pl.ds(pl.multiple_of(x * nw, nw), nw)
             res = lax.dot_general(
                 wr[pl.ds(first, count)].reshape(count * MC, width), tv[t, where, :],
@@ -225,7 +229,7 @@
             )
             return carry
 
-        lax.fori_loop(0, KT * 4, far_z, 0)
+        lax.fori_loop(0, KT * 2, far_z, 0)
         if full:
             pairs(c, 2, lambda i, s: idx[1, i, s], r2, 0)
             pairs(c, 1, lambda i, s: idx[0, i, s], r1, 0)

time: 44 us -> 41.6 us (0.945)
  the two profiles are of different devices: /device:TPU:5 before, /device:TPU:0 now
where the time goes in v3:
time: 41.6 us; the launch traced here: 41.3 us
  Pallas kernels  37.3 us (90%)
  local copies, waits for them, and re-layouts  2.49 us (6%)
  other arithmetic  1.51 us (4%)
    pallas_call x1, Pallas kernels, on_device(): pl.pallas_call(functools.partial(kernel, states, members, slots), out_sha...  37.3 us
    unnamed x1, local copies, waits for them, and re-layouts  1.3 us

profile of v3, /device:TPU:0, one launch (start us, length us, event | category | flops | bytes accessed | tf_op | source)
XLA Modules:
  0.0 41.3 jit_solution(10713303719512183715)
XLA Ops:
  0.0 0.7 %iota_compare_fusion = pred[8,12]{1,0:T(8,128)(4,1)S(1)} fusion(s32[8]{0:T(128)} %param.11), kind=kLoop, calls=%fused_computation.19 | loop fusion | flops 96 | bytes 128 | tf_op jit(solution)/shard_map/lt | solution.py:283
  0.7 0.8 %select_bitcast_fusion.1 = (s32[1,8,12]{2,1,0:T(8,128)S(1)}, s32[8,12]{1,0:T(8,128)S(1)}, s32[1,8,12]{2,1,0:T(8,128)S(1)}) fusion(s32[8,12]{1,0:T(8,128)} %param.9, s32[8,12]{1,0:T(8,128)} %param.10, s32[]{:T(128)S(6)} %sub.22, s32[]{:T(128)S(6)} %axis_index.15, s32[8]{0:T(128)} %param.11), kind=kLoop, calls=%fused_computation.16 | loop fusion | flops 4896 | bytes 1960 | tf_op jit(solution)/shard_map/stack | solution.py:292
  1.5 0.6 %pad.9.tabs = s32[2,8,128]{2,1,0:T(8,128)} pad(s32[2,8,12]{2,1,0:T(8,128)S(1)} %add_select_fusion, s32[]{:T(128)} %constant.55.clone.1), padding=0_0x0_0x0_116 | pad | bytes 8964 | tf_op jit(solution)/shard_map/jit(_pad)/pad | solution.py:293
  2.1 0.6 %pad.8.tab0_hbm = s32[8,128]{1,0:T(8,128)} pad(s32[8,12]{1,0:T(8,128)S(1)} %get-tuple-element.6, s32[]{:T(128)} %constant.55.clone.1), padding=0_0x0_116 | pad | bytes 4484 | tf_op jit(solution)/shard_map/jit(_pad)/pad | solution.py:289
  2.7 37.3 %shard_map.73 = f32[8,256]{1,0:T(8,128)} custom-call(s32[8,128]{1,0:T(8,128)} %pad.8.tab0_hbm, s32[2,8,128]{2,1,0:T(8,128)} %pad.9.tabs, s32[64,128]{1,0:T(8,128)} %bitcast.6, f32[64,128]{1,0:T(8,128)} %bitcast.7, bf16[8,64,1024]{2,1,0:T(8,128)(2,1)} %anom.1, bf16[2,1024,1024]{2,1,0:T(8,128)(2,1)} %tapers.1), custom_call_target="tpu_custom_call" | custom-call | tf_op jit(solution)/shard_map/pallas_call | solution.py:300
  40.0 1.3 %copy.9 = f32[8,256]{1,0:T(8,128)} copy(f32[8,256]{1,0:T(8,128)} %shard_map.73) | data formatting | bytes 16384
  (1 shorter events, 0.0 us)
